TPU v7x, 32 devices: a whole 2x2x4 slice. The times are simulated.
32 devices in a mesh: parts: 2 (over y), seq: 4 (over z), chan: 4 (over x, core).
Axes of the slice: x: 2, y: 2, z: 4, core: 2. Of those that a mesh axis runs over, the one named last changes fastest.
Arguments:
- x_tokens: bfloat16 [64, 8192], P(('parts', 'seq'), 'chan'), parts along dimension 0, may hold values from -6 to 6
- norm_gain: float32 [8192], P('chan'), may hold values from 0.5 to 1.5
- w_in: bfloat16 [3, 8192, 8192], P(None, 'seq', 'chan'), may hold values from -0.0625 to 0.0625
- short_filter: float32 [3, 3, 8192], P(None, None, 'seq'), may hold values from -3 to 3
- se_filter: float32 [7, 512], P(None, 'seq'), may hold values from -2 to 2
- w_out: bfloat16 [8192, 8192], P('seq'), may hold values from -0.0625 to 0.0625
Outputs:
- mixed_out: bfloat16 [64, 8192], P(('parts', 'chan'), 'seq'), parts along dimension 0
There are 2 independent parts, one for each index of `parts`. A program takes and returns all parts, laid end to end along the dimension named above; an argument that names none is the same for every part. Nothing has to cross between parts.
All inputs are finite; a program needn't handle non-finite values.
Results may differ from a plain program's by a relative error of at most 0.0086.
Values may be sent and summed in bfloat16 or wider, within the bound.
No kernel may reach another device: no remote copies, remote signals or barrier semaphores. Data moves between devices by JAX's collectives and lax.ppermute only.
A program may use at most 128 MiB of HBM per device.

v0:
```python
import jax
import jax.numpy as jnp
from jax import lax
from jax.sharding import PartitionSpec as P

D = 8192
GROUP = 16
epsilon = 1e-06


def from_behind(value, axis, steps):
    count = lax.axis_size(axis)
    leading, last = (max(0, -steps), min(count, count - steps))
    return lax.ppermute(value, axis, [(source, source + steps) for source in range(leading, last)])


def mixer(extended, short_taps, long_taps):
    wide = extended.astype(jnp.float32)
    row_count = wide.shape[0]
    featured = sum(
        (short_taps[offset] * wide[2 - offset : row_count - offset] for offset in range(3))
    )
    queries = featured[:, 0]
    product = featured[:, 1] * featured[:, 2]
    length = product.shape[0]
    filtered = sum(
        (long_taps[offset] * product[6 - offset : length - offset] for offset in range(7))
    )
    return (queries[6:] * filtered).astype(jnp.bfloat16)


def contract_last(left, right):
    return lax.dot_general(
        left, right, (((1,), (1,)), ((), ())), preferred_element_type=jnp.float32
    )


def shards(x_tokens, norm_gain, w_in, short_filter, se_filter, w_out):
    wide = x_tokens.astype(jnp.float32)
    local_squares = jnp.sum(wide * wide, axis=1, keepdims=True)
    total_squares = lax.psum(local_squares, "chan")
    factor = lax.rsqrt(total_squares / D + epsilon)
    normed = (wide * factor * norm_gain).astype(jnp.bfloat16)
    columns = w_in.shape[1]
    flat_in = w_in.reshape(3 * columns, w_in.shape[2])
    piece = lax.all_gather(normed, "seq", axis=0, tiled=True)
    partial_terms = contract_last(piece, flat_in).reshape(piece.shape[0], 3, columns)
    long_full = jnp.repeat(se_filter, GROUP, axis=1)
    mine = lax.psum_scatter(partial_terms, "chan", scatter_dimension=0, tiled=True).astype(
        jnp.bfloat16
    )
    previous = from_behind(mine[-8:], "chan", 1)
    extended = jnp.concatenate([previous, mine], axis=0)
    gated = mixer(extended, short_filter, long_full)
    result = contract_last(lax.all_gather(gated, "seq", axis=1, tiled=True), w_out)
    return result.astype(jnp.bfloat16)


def solution(mesh):
    placed = (
        P(("parts", "seq"), "chan"),
        P("chan"),
        P(None, "seq", "chan"),
        P(None, None, "seq"),
        P(None, "seq"),
        P("seq", None),
    )
    return jax.shard_map(
        shards, mesh=mesh, in_specs=placed, out_specs=P(("parts", "chan"), "seq"), check_vma=False
    )
```

profile of v0, /device:TPU:0, one launch (start us, length us, event | category | flops | bytes accessed | tf_op | source)
XLA Modules:
  0.0 107.5 jit_solution(7954886832939469192)
XLA Ops:
  6.5 0.9 fusion.4
  7.4 8.4 %psum.7 = f32[8,1]{0,1:T(1,128)S(1)} all-reduce(f32[8,1]{0,1:T(1,128)S(1)} %bitcast.89), channel_id=1, replica_groups=mesh['parts'=2,'seq'=4,'chan'=4] {'chan'}, use_global_device_ids=true, to_apply=%region_1.0 | all-reduce | flops 8 | bytes 64 | tf_op jit(solution)/shard_map/psum | solution.py:41
  15.8 0.8 fusion.6
  16.6 13.6 %all_gather.6 = bf16[32,2048]{1,0:T(8,128)(2,1)S(1)} all-gather(bf16[8,2048]{1,0:T(8,128)(2,1)S(1)} %fusion.6), channel_id=1, replica_groups=mesh['parts'=2,'seq'=4,'chan'=4] {'seq'}, dimensions={0}, use_global_device_ids=true | all-gather | bytes 163840 | tf_op jit(solution)/shard_map/all_gather | solution.py:46
  30.2 13.0 %fusion.2 = f32[32,3,2048]{2,0,1:T(8,128)} fusion(bf16[3,2048,2048]{2,1,0:T(8,128)(2,1)} %param.8, bf16[32,2048]{1,0:T(8,128)(2,1)S(1)} %all_gather.6), kind=kOutput, calls=%fused_computation.8 | convolution fusion | flops 805306368 | bytes 26083328 | tf_op jit(solution)/shard_map/dot_general | solution.py:33
  43.3 0.8 slice_bitcast_fusion.10
  44.1 22.8 %reduce-scatter.2.cloned.1.call-done = f32[8,3,2048]{2,0,1:T(8,128)} async-done(((f32[32,3,2048]{2,0,1:T(8,128)}), f32[8,3,2048]{2,0,1:T(8,128)}) %reduce-scatter.2.cloned.1.call-update) | async-done | bytes 196624 | tf_op jit(solution)/shard_map/reduce_scatter | solution.py:49
  66.9 0.9 convert_element_type.20
  67.9 1.6 %collective-permute-start = (bf16[8,3,2048]{2,0,1:T(8,128)(2,1)S(1)}, bf16[8,3,2048]{2,0,1:T(8,128)(2,1)S(1)}, u32[]{:S(2)}, u32[]{:S(2)}) collective-permute-start(bf16[8,3,2048]{2,0,1:T(8,128)(2,1)S(1)} %convert_element_type.20), channel_id=1, source_target_pairs={{0,1},{1,2},{2,3},{4,5},{5,6},{6,7},{8,9},{9,10},{10,11},{12,13},{... | collective-permute-start | bytes 294920 | tf_op jit(solution)/shard_map/ppermute | solution.py:14
  69.4 0.9 slice_bitcast_fusion.17
  70.4 0.1 broadcast_in_dim.34
  70.5 0.1 broadcast_in_dim.35
  70.6 0.1 broadcast_in_dim.36
  70.6 0.1 broadcast_in_dim.37
  70.8 0.1 broadcast_in_dim.39
  70.9 0.1 broadcast_in_dim.40
  71.0 0.1 broadcast_in_dim.41
  71.1 0.1 broadcast_in_dim.43
  71.3 0.1 broadcast_in_dim.45
  71.5 0.1 broadcast_in_dim.47
  71.6 0.1 fusion
  71.8 0.1 fusion.10
  71.8 13.7 %all_gather.7 = bf16[8,8192]{1,0:T(8,128)(2,1)S(1)} all-gather(bf16[8,2048]{1,0:T(8,128)(2,1)S(1)} %fusion.10), channel_id=1, replica_groups=mesh['parts'=2,'seq'=4,'chan'=4] {'seq'}, dimensions={1}, use_global_device_ids=true | all-gather | bytes 163840 | tf_op jit(solution)/shard_map/all_gather | solution.py:55
  85.5 15.1 %convolution_convert_fusion = bf16[8,2048]{1,0:T(8,128)(2,1)} fusion(bf16[8,8192]{1,0:T(8,128)(2,1)S(1)} %all_gather.7, bf16[2048,8192]{1,0:T(8,128)(2,1)} %param.11), kind=kOutput, calls=%fused_computation | convolution fusion | flops 268451840 | bytes 33718272 | tf_op jit(solution)/shard_map/dot_general | solution.py:33
  (10 shorter events, 0.4 us)
Async XLA Ops:
  6.5 60.4 %reduce-scatter.2.cloned.1.call-start = ((), (), s32[]{:S(2)}) async-start(), calls=%async_computation.1 | async-start | bytes 983040 | tf_op jit(solution)/shard_map/reduce_scatter | solution.py:49
  67.9 3.7 %collective-permute-start = (bf16[8,3,2048]{2,0,1:T(8,128)(2,1)S(1)}, bf16[8,3,2048]{2,0,1:T(8,128)(2,1)S(1)}, u32[]{:S(2)}, u32[]{:S(2)}) collective-permute-start(bf16[8,3,2048]{2,0,1:T(8,128)(2,1)S(1)} %convert_element_type.20), channel_id=1, source_target_pairs={{0,1},{1,2},{2,3},{4,5},{5,6},{6,7},{8,9},{9,10},{10,11},{12,13},{... | collective-permute-start | bytes 294920 | tf_op jit(solution)/shard_map/ppermute | solution.py:14
Sparse Core Ops, SparseCore 0:
  43.4 23.4 reduce-scatter.1
where the time goes:
time: 108 us; the launch traced here: 107 us
  blocking collectives  35.7 us (33%)
  matrix products  28.1 us (26%)
  waiting for transfers between devices  22.8 us (21%)
  between operations  13.4 us (12%)
  local copies, waits for them, and re-layouts  2.93 us (3%)
  other arithmetic  2.92 us (3%)
  starting transfers between devices  1.56 us (1%)
    dot_general x2, matrix products, contract_last(): lax.dot_general(left, right, (((1,), (1,)), ((), ())), preferred_element_...  28.1 us
    reduce_scatter x1, waiting for transfers between devices, shards(): lax.psum_scatter(partial_terms, 'chan', scatter_dimension=0, tiled=True)  22.8 us
    all_gather x1, blocking collectives, shards(): lax.all_gather(gated, 'seq', axis=1, tiled=True)  13.7 us
    all_gather x1, blocking collectives, shards(): piece = lax.all_gather(normed, 'seq', axis=0, tiled=True)  13.6 us
    psum x1, blocking collectives, shards(): total_squares = lax.psum(local_squares, 'chan')  8.36 us
  transfers between devices with their start and end apart: 2, of which 1 were waited for; matrix products, arithmetic and copies ran while one was open for 3% of the time, Pallas kernels for 0%

commit v1 on v0

--- a/solution.py
+++ b/solution.py
@@ -52,7 +52,7 @@
     previous = from_behind(mine[-8:], "chan", 1)
     extended = jnp.concatenate([previous, mine], axis=0)
     gated = mixer(extended, short_filter, long_full)
-    result = contract_last(lax.all_gather(gated, "seq", axis=1, tiled=True), w_out)
+    result = contract_last(jnp.concatenate(lax.all_gather(gated, "seq"), axis=1), w_out)
     return result.astype(jnp.bfloat16)
 
 

time: 108 us -> 108 us (level)
  no operation moved by 1% of the time
where the time goes in v1:
time: 108 us; the launch traced here: 107 us
  blocking collectives  35.7 us (33%)
  matrix products  28.1 us (26%)
  waiting for transfers between devices  22.8 us (21%)
  between operations  13.4 us (12%)
  local copies, waits for them, and re-layouts  2.93 us (3%)
  other arithmetic  2.92 us (3%)
  starting transfers between devices  1.56 us (1%)
    dot_general x2, matrix products, contract_last(): lax.dot_general(left, right, (((1,), (1,)), ((), ())), preferred_element_...  28.1 us
    reduce_scatter x1, waiting for transfers between devices, shards(): lax.psum_scatter(partial_terms, 'chan', scatter_dimension=0, tiled=True)  22.8 us
    all_gather x1, blocking collectives, shards(): lax.all_gather(gated, 'seq')  13.7 us
    all_gather x1, blocking collectives, shards(): piece = lax.all_gather(normed, 'seq', axis=0, tiled=True)  13.6 us
    psum x1, blocking collectives, shards(): total_squares = lax.psum(local_squares, 'chan')  8.36 us
  transfers between devices with their start and end apart: 2, of which 1 were waited for; matrix products, arithmetic and copies ran while one was open for 3% of the time, Pallas kernels for 0%

profile of v1, /device:TPU:0, one launch (start us, length us, event | category | flops | bytes accessed | tf_op | source)
XLA Modules:
  0.0 107.5 jit_solution(4308337782355564800)
XLA Ops:
  6.5 0.9 fusion.4
  7.4 8.4 %psum.7 = f32[8,1]{0,1:T(1,128)S(1)} all-reduce(f32[8,1]{0,1:T(1,128)S(1)} %bitcast.95), channel_id=1, replica_groups=mesh['parts'=2,'seq'=4,'chan'=4] {'chan'}, use_global_device_ids=true, to_apply=%region_1.0 | all-reduce | flops 8 | bytes 64 | tf_op jit(solution)/shard_map/psum | solution.py:41
  15.8 0.8 fusion.6
  16.6 13.6 %all_gather.9 = bf16[32,2048]{1,0:T(8,128)(2,1)S(1)} all-gather(bf16[8,2048]{1,0:T(8,128)(2,1)S(1)} %fusion.6), channel_id=1, replica_groups=mesh['parts'=2,'seq'=4,'chan'=4] {'seq'}, dimensions={0}, use_global_device_ids=true | all-gather | bytes 163840 | tf_op jit(solution)/shard_map/all_gather | solution.py:46
  30.2 13.0 %fusion.2 = f32[32,3,2048]{2,0,1:T(8,128)} fusion(bf16[3,2048,2048]{2,1,0:T(8,128)(2,1)} %param.8, bf16[32,2048]{1,0:T(8,128)(2,1)S(1)} %all_gather.9), kind=kOutput, calls=%fused_computation.8 | convolution fusion | flops 805306368 | bytes 26083328 | tf_op jit(solution)/shard_map/dot_general | solution.py:33
  43.3 0.8 slice_bitcast_fusion.10
  44.1 22.8 %reduce-scatter.2.cloned.1.call-done = f32[8,3,2048]{2,0,1:T(8,128)} async-done(((f32[32,3,2048]{2,0,1:T(8,128)}), f32[8,3,2048]{2,0,1:T(8,128)}) %reduce-scatter.2.cloned.1.call-update) | async-done | bytes 196624 | tf_op jit(solution)/shard_map/reduce_scatter | solution.py:49
  66.9 0.9 convert_element_type.20
  67.9 1.6 %collective-permute-start = (bf16[8,3,2048]{2,0,1:T(8,128)(2,1)S(1)}, bf16[8,3,2048]{2,0,1:T(8,128)(2,1)S(1)}, u32[]{:S(2)}, u32[]{:S(2)}) collective-permute-start(bf16[8,3,2048]{2,0,1:T(8,128)(2,1)S(1)} %convert_element_type.20), channel_id=1, source_target_pairs={{0,1},{1,2},{2,3},{4,5},{5,6},{6,7},{8,9},{9,10},{10,11},{12,13},{... | collective-permute-start | bytes 294920 | tf_op jit(solution)/shard_map/ppermute | solution.py:14
  69.4 0.9 slice_bitcast_fusion.17
  70.4 0.1 broadcast_in_dim.34
  70.5 0.1 broadcast_in_dim.35
  70.6 0.1 broadcast_in_dim.36
  70.6 0.1 broadcast_in_dim.37
  70.8 0.1 broadcast_in_dim.39
  70.9 0.1 broadcast_in_dim.40
  71.0 0.1 broadcast_in_dim.41
  71.1 0.1 broadcast_in_dim.43
  71.3 0.1 broadcast_in_dim.45
  71.5 0.1 broadcast_in_dim.47
  71.6 0.1 fusion
  71.8 0.1 fusion.10
  71.8 13.7 %all-gather = bf16[32,2048]{1,0:T(8,128)(2,1)S(1)} all-gather(bf16[8,2048]{1,0:T(8,128)(2,1)S(1)} %fusion.10), channel_id=2, replica_groups=mesh['parts'=2,'seq'=4,'chan'=4] {'seq'}, dimensions={0}, use_global_device_ids=true | all-gather | bytes 163840 | tf_op jit(solution)/shard_map/all_gather | solution.py:55
  85.5 15.1 %convolution_convert_fusion = bf16[8,2048]{1,0:T(8,128)(2,1)} fusion(bf16[8,8192]{1,0:T(8,128)(2,1)S(1)} %bitcast.94, bf16[2048,8192]{1,0:T(8,128)(2,1)} %param.11), kind=kOutput, calls=%fused_computation | convolution fusion | flops 268451840 | bytes 33718272 | tf_op jit(solution)/shard_map/dot_general | solution.py:33
  (10 shorter events, 0.4 us)
Async XLA Ops:
  6.5 60.4 %reduce-scatter.2.cloned.1.call-start = ((), (), s32[]{:S(2)}) async-start(), calls=%async_computation.1 | async-start | bytes 983040 | tf_op jit(solution)/shard_map/reduce_scatter | solution.py:49
  67.9 3.7 %collective-permute-start = (bf16[8,3,2048]{2,0,1:T(8,128)(2,1)S(1)}, bf16[8,3,2048]{2,0,1:T(8,128)(2,1)S(1)}, u32[]{:S(2)}, u32[]{:S(2)}) collective-permute-start(bf16[8,3,2048]{2,0,1:T(8,128)(2,1)S(1)} %convert_element_type.20), channel_id=1, source_target_pairs={{0,1},{1,2},{2,3},{4,5},{5,6},{6,7},{8,9},{9,10},{10,11},{12,13},{... | collective-permute-start | bytes 294920 | tf_op jit(solution)/shard_map/ppermute | solution.py:14
Sparse Core Ops, SparseCore 0:
  43.4 23.4 reduce-scatter.1
